TPU v7x, 32 devices: a whole 2x2x4 slice. The times are simulated.
32 devices in a mesh: team: 2 (over x), blk: 4 (over z), head: 4 (over y, core).
Axes of the slice: x: 2, y: 2, z: 4, core: 2. Of those that a mesh axis runs over, the one named last changes fastest.
Arguments:
- queries: bfloat16 [1024, 8, 8, 128], P('blk', 'head', 'team'), may hold values from -40 to 40
- features: bfloat16 [1024, 8192], P('blk', ('team', 'head')), may hold values from -6 to 6
- adapter_down: bfloat16 [4, 8192, 64], P(None, ('team', 'head')), may hold values from -0.0625 to 0.0625
- adapter_key_up: bfloat16 [4, 64, 8, 128], P(None, None, 'head'), may hold values from -0.75 to 0.75
- adapter_value_up: bfloat16 [4, 64, 8, 128], P(None, None, 'head'), may hold values from -0.75 to 0.75
- base_key: bfloat16 [1024, 8, 128], P('blk', 'head'), may hold values from -6 to 6
- base_value: bfloat16 [1024, 8, 128], P('blk', 'head'), may hold values from -24 to 24
- prefix_key: bfloat16 [2048, 8, 128], P('blk', 'head'), may hold values from -7 to 7
- prefix_value: bfloat16 [2048, 8, 128], P('blk', 'head'), may hold values from -24 to 24
- adapter_ids: int32 [4], replicated, may hold values from 0 to 3
- block_order: int32 [4], replicated, may hold values from 0 to 15
Outputs:
- attended: bfloat16 [1024, 8, 8, 128], P('blk', 'head', 'team')
All inputs are finite; a program needn't handle non-finite values.
Results may differ from a plain program's by a relative error of at most 0.011.
Values may be sent and summed in bfloat16 or wider, within the bound.
No kernel may reach another device: no remote copies, remote signals or barrier semaphores. Data moves between devices by JAX's collectives and lax.ppermute only.
A program may use at most 64 MiB of HBM per device.

v0:
```python
import math
import jax
import jax.numpy as jnp
from jax import lax
from jax.sharding import PartitionSpec as P

NEG_FILL = -1e30


def block_length(row_count):
    for candidate in range(min(row_count, 1024), 0, -1):
        if row_count % candidate == 0:
            return candidate
    return row_count


def key_positions(row_count, shard_rows, prefix_dev, query_dev, block_order, block_count):
    row_index = jnp.arange(row_count, dtype=jnp.int32)
    holder = row_index // shard_rows
    within = row_index - holder * shard_rows
    block_ids = jnp.arange(block_count, dtype=jnp.int32)
    holder_order = jnp.sum(
        jnp.where(holder[:, None] == block_ids[None, :], block_order[None, :], 0), axis=1
    )
    later = prefix_dev * block_count + holder_order * query_dev + within - prefix_dev
    return jnp.where(within < prefix_dev, holder * prefix_dev + within, later)


def attend(running, query_rows, query_pos, key_rows, value_rows, key_pos):
    row_count = key_rows.shape[0]
    block_rows = block_length(row_count)
    key_blocks = row_count // block_rows
    kv_heads = key_rows.shape[1]
    head_dim = key_rows.shape[2]
    score_scale = 1.0 / math.sqrt(head_dim)
    latest = jnp.max(query_pos)
    key_split = key_rows.reshape((key_blocks, block_rows, kv_heads, head_dim))
    value_split = value_rows.reshape((key_blocks, block_rows, kv_heads, head_dim))
    pos_split = key_pos.reshape((key_blocks, block_rows))

    def advance(carried, block_data):
        block_keys, block_values, block_pos = block_data

        def compute(previous):
            row_max, row_sum, weighted = previous
            scores = (
                jnp.einsum(
                    "tkgd,skd->kgts", query_rows, block_keys, preferred_element_type=jnp.float32
                )
                * score_scale
            )
            visible = block_pos[None, None, None, :] <= query_pos[None, None, :, None]
            scores = jnp.where(visible, scores, NEG_FILL)
            new_max = jnp.maximum(row_max, jnp.max(scores, axis=-1))
            weights = jnp.where(visible, jnp.exp(scores - new_max[..., None]), 0.0)
            factor = jnp.exp(row_max - new_max)
            row_sum = row_sum * factor + jnp.sum(weights, axis=-1)
            product = jnp.einsum(
                "kgts,skd->kgtd",
                weights.astype(jnp.bfloat16),
                block_values,
                preferred_element_type=jnp.float32,
            )
            weighted = weighted * factor[..., None] + product
            return (new_max, row_sum, weighted)

        return (lax.cond(jnp.min(block_pos) > latest, lambda kept: kept, compute, carried), None)

    result, _ = lax.scan(advance, running, (key_split, value_split, pos_split))
    return result


def on_device(
    queries,
    features,
    adapter_down,
    adapter_key_up,
    adapter_value_up,
    base_key,
    base_value,
    prefix_key,
    prefix_value,
    adapter_ids,
    block_order,
):
    block_count = lax.axis_size("blk")
    my_block = lax.axis_index("blk")
    query_dev = queries.shape[0]
    kv_heads = queries.shape[1]
    group_dev = queries.shape[2]
    head_dim = queries.shape[3]
    prefix_dev = prefix_key.shape[0]
    rank_width = adapter_down.shape[2]
    shard_rows = prefix_dev + query_dev
    chosen = adapter_ids[my_block]
    down_rows = lax.dynamic_index_in_dim(adapter_down, chosen, 0, keepdims=False)
    partial_latent = jnp.dot(features, down_rows, preferred_element_type=jnp.float32)
    latent = lax.psum(partial_latent, ("team", "head")).astype(jnp.bfloat16)

    def expand(up_table, base_rows):
        up_rows = lax.dynamic_index_in_dim(up_table, chosen, 0, keepdims=False).reshape(
            rank_width, kv_heads * head_dim
        )
        delta = jnp.dot(latent, up_rows, preferred_element_type=jnp.float32).reshape(
            query_dev, kv_heads, head_dim
        )
        return (base_rows.astype(jnp.float32) + delta).astype(jnp.bfloat16)

    key_rows = jnp.concatenate([prefix_key, expand(adapter_key_up, base_key)], axis=0)
    value_rows = jnp.concatenate([prefix_value, expand(adapter_value_up, base_value)], axis=0)
    prefix_total = prefix_dev * block_count
    offsets = jnp.arange(query_dev, dtype=jnp.int32)
    query_pos = prefix_total + block_order[my_block] * query_dev + offsets
    initial = (
        jnp.full((kv_heads, group_dev, query_dev), NEG_FILL, jnp.float32),
        jnp.zeros((kv_heads, group_dev, query_dev), jnp.float32),
        jnp.zeros((kv_heads, group_dev, query_dev, head_dim), jnp.float32),
    )
    key_piece = lax.all_gather(key_rows, "blk", axis=0, tiled=True)
    value_piece = lax.all_gather(value_rows, "blk", axis=0, tiled=True)
    piece_pos = key_positions(
        key_piece.shape[0], shard_rows, prefix_dev, query_dev, block_order, block_count
    )
    row_max, row_sum, weighted = attend(
        initial, queries, query_pos, key_piece, value_piece, piece_pos
    )
    result = weighted / row_sum[..., None]
    return result.transpose(2, 0, 1, 3).astype(jnp.bfloat16)


def solution(mesh):
    placed = (
        P("blk", "head", "team", None),
        P("blk", ("team", "head")),
        P(None, ("team", "head"), None),
        P(None, None, "head", None),
        P(None, None, "head", None),
        P("blk", "head", None),
        P("blk", "head", None),
        P("blk", "head", None),
        P("blk", "head", None),
        P(),
        P(),
    )
    return jax.shard_map(
        on_device,
        mesh=mesh,
        in_specs=placed,
        out_specs=P("blk", "head", "team", None),
        check_vma=False,
    )
```

profile of v0, /device:TPU:0, one launch (start us, length us, event | category | flops | bytes accessed | tf_op | source)
XLA Modules:
  0.0 160.4 jit_solution(10820601032562232662)
XLA Ops:
  6.5 0.0 copy-start
  6.5 0.0 all-gather.3.cloned.1.call-start
  6.5 1.3 dynamic_slice.39
  9.8 0.0 copy-done
  9.8 1.2 convolution_bitcast_fusion
  11.0 26.0 %psum.7 = bf16[256,64]{0,1:T(8,128)(2,1)S(1)} all-reduce(f32[256,64]{0,1:T(8,128)S(1)} %convolution_bitcast_fusion), channel_id=1, replica_groups=mesh['team'=2,'blk'=4,'head'=4] {'team','head'}, use_global_device_ids=true, to_apply=%region_0.1 | all-reduce | flops 16384 | bytes 98304 | tf_op jit(solution)/shard_map/psum | solution.py:98
  37.0 1.0 copy.35
  38.0 0.8 constant_dynamic-slice_fusion.1
  38.8 1.1 fusion.21
  39.9 0.8 pad_maximum_fusion
  40.7 0.0 all-gather.3.cloned.1.call-update
  40.7 0.0 all-gather.5.cloned.1.call-start
  40.8 1.0 copy.38
  41.8 1.1 fusion.22
  42.9 0.8 pad_maximum_fusion.1
  43.6 0.0 all-gather.5.cloned.1.call-update
  43.7 1.2 dynamic_slice.38
  45.5 0.6 add_reduce_fusion
  46.1 1.1 copy.40
  47.2 0.8 select_reduce_fusion
  48.1 29.3 %all-gather.3.cloned.1.call-done = bf16[3072,2,128]{2,0,1:T(8,128)(2,1)} async-done(((bf16[768,2,128]{2,0,1:T(8,128)(2,1)}), bf16[3072,2,128]{2,0,1:T(8,128)(2,1)}) %all-gather.3.cloned.1.call-update) | async-done | bytes 1572880 | tf_op jit(solution)/shard_map/all_gather | solution.py:119
  77.4 1.5 copy.39
  78.9 36.0 %all-gather.5.cloned.1.call-done = bf16[3072,2,128]{2,0,1:T(8,128)(2,1)} async-done(((bf16[768,2,128]{2,0,1:T(8,128)(2,1)}), bf16[3072,2,128]{2,0,1:T(8,128)(2,1)}) %all-gather.5.cloned.1.call-update) | async-done | bytes 1572880 | tf_op jit(solution)/shard_map/all_gather | solution.py:120
  114.9 2.7 %copy.41 = bf16[3,1024,2,128]{3,1,2,0:T(8,128)(2,1)} copy(bf16[3,1024,2,128]{3,1,0,2:T(8,128)(2,1)} %bitcast.83) | data formatting | bytes 3145728
  117.6 1.0 broadcast_in_dim.56
  118.6 31.8 %while.15 = (s32[]{:T(128)}, f32[2,4,256]{2,1,0:T(4,128)S(1)}, f32[2,4,256]{2,1,0:T(4,128)S(1)}, f32[2,4,256,128]{3,2,1,0:T(8,128)}, s32[3,1024]{1,0:T(4,128)S(1...) while((s32[]{:T(128)}, f32[2,4,256]{2,1,0:T(4,128)S(1)}, ...), condition=%wide.region_9.10_spmd.clone, body=%wide.region_3.9_spmd.clone.sunk | while | flops 1101796608 | bytes 38421312 | solution.py:69
  118.6 0.6 fusion.45
  120.5 8.7 %conditional.3 = (f32[2,4,256]{2,1,0:T(4,128)S(1)}, f32[2,4,256]{2,1,0:T(4,128)S(1)}, f32[2,4,256,128]{3,2,1,0:T(8,128)}) conditional(s32[]{:T(128)} %convert_element_type.57, (s32[1,1024]{1,0:T(1,128)S(1)}, s32[]{:T(128)}, bf16[3,1024,2,128]{3,1,2,0:T(8,128)(2,1)S(1)}, s32[]{:T(128)}, bf16[256,2,4,128]{3,0,2,1:T(8,128)(2,1)S(1)}, ...), branch_computations={%region_5.7_spmd, %region_8.8_spmd} | conditional | flops 1101795584 | bytes 38395480 | solution.py:67
  120.5 0.2 broadcast_compare_fusion
  120.7 0.0 copy-start.1
  120.7 1.4 fusion.2
  122.2 2.0 %fusion.4 = f32[2,4,256]{2,1,0:T(4,128)S(1)} fusion(f32[2,1024,256,4]{2,1,3,0:T(8,128)S(1)} %get-tuple-element.228, f32[2,4,256]{2,1,0:T(4,128)S(1)} %max.4, pred[256,1024]{0,1:T(8,128)(4,1)S(1)} %broadcast_compare_fusion), kind=kLoop, calls=%fused_computation.5 | loop fusion | flops 10483712 | bytes 8667136 | tf_op jit(solution)/shard_map/while/body/eval_jaxpr/cond/branch_0_fun/reduce_sum | solution.py:57
  124.2 0.0 copy-done.1
  124.2 4.0 %fusion.8 = f32[2,4,256,128]{3,2,1,0:T(8,128)S(1)} fusion(f32[2,1024,256,4]{2,1,3,0:T(8,128)S(1)} %get-tuple-element.228, f32[2,4,256]{2,1,0:T(4,128)S(1)} %max.4, pred[256,1024]{0,1:T(8,128)(4,1)S(1)} %broadcast_compare_fusion, f32[2,4,256,128]{3,2,1,0:T(8,128)S(1)} %copy-done.1, bf16[3,1024,2,128]{3,1,2,0:T(8,128)(2,1)} %get-tuple-element.125, ...), kind=kOutput, calls=%fused_computation.8 | convolution fusion | flops 547880960 | bytes 11289088 | tf_op jit(solution)/shard_map/while/body/eval_jaxpr/cond/branch_0_fun/kgts,skd->kgtd/dot_general | solution.py:58
  128.3 0.0 copy-start.2
  128.3 1.0 copy-done.2
  129.2 0.6 fusion.45
  131.1 8.7 %conditional.3 = (f32[2,4,256]{2,1,0:T(4,128)S(1)}, f32[2,4,256]{2,1,0:T(4,128)S(1)}, f32[2,4,256,128]{3,2,1,0:T(8,128)}) conditional(s32[]{:T(128)} %convert_element_type.57, (s32[1,1024]{1,0:T(1,128)S(1)}, s32[]{:T(128)}, bf16[3,1024,2,128]{3,1,2,0:T(8,128)(2,1)S(1)}, s32[]{:T(128)}, bf16[256,2,4,128]{3,0,2,1:T(8,128)(2,1)S(1)}, ...), branch_computations={%region_5.7_spmd, %region_8.8_spmd} | conditional | flops 1101795584 | bytes 38395480 | solution.py:67
  131.1 0.2 broadcast_compare_fusion
  131.3 0.0 copy-start.1
  131.3 1.4 fusion.2
  132.8 2.0 %fusion.4 = f32[2,4,256]{2,1,0:T(4,128)S(1)} fusion(f32[2,1024,256,4]{2,1,3,0:T(8,128)S(1)} %get-tuple-element.228, f32[2,4,256]{2,1,0:T(4,128)S(1)} %max.4, pred[256,1024]{0,1:T(8,128)(4,1)S(1)} %broadcast_compare_fusion), kind=kLoop, calls=%fused_computation.5 | loop fusion | flops 10483712 | bytes 8667136 | tf_op jit(solution)/shard_map/while/body/eval_jaxpr/cond/branch_0_fun/reduce_sum | solution.py:57
  134.8 0.0 copy-done.1
  134.8 4.0 %fusion.8 = f32[2,4,256,128]{3,2,1,0:T(8,128)S(1)} fusion(f32[2,1024,256,4]{2,1,3,0:T(8,128)S(1)} %get-tuple-element.228, f32[2,4,256]{2,1,0:T(4,128)S(1)} %max.4, pred[256,1024]{0,1:T(8,128)(4,1)S(1)} %broadcast_compare_fusion, f32[2,4,256,128]{3,2,1,0:T(8,128)S(1)} %copy-done.1, bf16[3,1024,2,128]{3,1,2,0:T(8,128)(2,1)} %get-tuple-element.125, ...), kind=kOutput, calls=%fused_computation.8 | convolution fusion | flops 547880960 | bytes 11289088 | tf_op jit(solution)/shard_map/while/body/eval_jaxpr/cond/branch_0_fun/kgts,skd->kgtd/dot_general | solution.py:58
  138.9 0.0 copy-start.2
  138.9 1.0 copy-done.2
  139.8 0.6 fusion.45
  141.7 8.7 %conditional.3 = (f32[2,4,256]{2,1,0:T(4,128)S(1)}, f32[2,4,256]{2,1,0:T(4,128)S(1)}, f32[2,4,256,128]{3,2,1,0:T(8,128)}) conditional(s32[]{:T(128)} %convert_element_type.57, (s32[1,1024]{1,0:T(1,128)S(1)}, s32[]{:T(128)}, bf16[3,1024,2,128]{3,1,2,0:T(8,128)(2,1)S(1)}, s32[]{:T(128)}, bf16[256,2,4,128]{3,0,2,1:T(8,128)(2,1)S(1)}, ...), branch_computations={%region_5.7_spmd, %region_8.8_spmd} | conditional | flops 1101795584 | bytes 38395480 | solution.py:67
  141.7 0.2 broadcast_compare_fusion
  141.9 0.0 copy-start.1
  141.9 1.4 fusion.2
  143.4 2.0 %fusion.4 = f32[2,4,256]{2,1,0:T(4,128)S(1)} fusion(f32[2,1024,256,4]{2,1,3,0:T(8,128)S(1)} %get-tuple-element.228, f32[2,4,256]{2,1,0:T(4,128)S(1)} %max.4, pred[256,1024]{0,1:T(8,128)(4,1)S(1)} %broadcast_compare_fusion), kind=kLoop, calls=%fused_computation.5 | loop fusion | flops 10483712 | bytes 8667136 | tf_op jit(solution)/shard_map/while/body/eval_jaxpr/cond/branch_0_fun/reduce_sum | solution.py:57
  145.4 0.0 copy-done.1
  145.4 4.0 %fusion.8 = f32[2,4,256,128]{3,2,1,0:T(8,128)S(1)} fusion(f32[2,1024,256,4]{2,1,3,0:T(8,128)S(1)} %get-tuple-element.228, f32[2,4,256]{2,1,0:T(4,128)S(1)} %max.4, pred[256,1024]{0,1:T(8,128)(4,1)S(1)} %broadcast_compare_fusion, f32[2,4,256,128]{3,2,1,0:T(8,128)S(1)} %copy-done.1, bf16[3,1024,2,128]{3,1,2,0:T(8,128)(2,1)} %get-tuple-element.125, ...), kind=kOutput, calls=%fused_computation.8 | convolution fusion | flops 547880960 | bytes 11289088 | tf_op jit(solution)/shard_map/while/body/eval_jaxpr/cond/branch_0_fun/kgts,skd->kgtd/dot_general | solution.py:58
  149.5 0.0 copy-start.2
  149.5 1.0 copy-done.2
  150.4 0.2 copy.42
  150.6 2.9 %fusion.24 = bf16[256,2,4,128]{3,2,1,0:T(4,128)(2,1)} fusion(f32[2,4,256]{1,0,2:T(2,128)S(1)} %copy.42, f32[2,4,256,128]{3,2,1,0:T(8,128)} %get-tuple-element.142), kind=kLoop, calls=%fused_computation.31 | loop fusion | flops 524288 | bytes 1581056 | tf_op jit(solution)/shard_map/convert_element_type | solution.py:128
  (21 shorter events, 0.1 us)
Async XLA Ops:
  6.5 3.2 %copy-start = (bf16[256,1024]{1,0:T(8,128)(2,1)S(1)}, bf16[256,1024]{1,0:T(8,128)(2,1)}, u32[]{:S(2)}) copy-start(bf16[256,1024]{1,0:T(8,128)(2,1)} %param.16) | copy-start | bytes 1572868
  6.5 70.8 %all-gather.3.cloned.1.call-start = ((), (), s32[]{:S(2)}) async-start(), calls=%async_computation | async-start | bytes 1966080 | tf_op jit(solution)/shard_map/all_gather | solution.py:119
  40.7 74.2 %all-gather.5.cloned.1.call-start = ((), (), s32[]{:S(2)}) async-start(), calls=%async_computation.1 | async-start | bytes 1966080 | tf_op jit(solution)/shard_map/all_gather | solution.py:120
  120.7 3.5 %copy-start.1 = (f32[2,4,256,128]{3,2,1,0:T(8,128)S(1)}, f32[2,4,256,128]{3,2,1,0:T(8,128)}, u32[]{:S(2)}) copy-start(f32[2,4,256,128]{3,2,1,0:T(8,128)} %get-tuple-element.124) | copy-start | bytes 3145732 | tf_op jit(solution)/shard_map/while/body/eval_jaxpr/cond
  128.3 1.0 copy-start.2
  131.3 3.5 %copy-start.1 = (f32[2,4,256,128]{3,2,1,0:T(8,128)S(1)}, f32[2,4,256,128]{3,2,1,0:T(8,128)}, u32[]{:S(2)}) copy-start(f32[2,4,256,128]{3,2,1,0:T(8,128)} %get-tuple-element.124) | copy-start | bytes 3145732 | tf_op jit(solution)/shard_map/while/body/eval_jaxpr/cond
  138.9 1.0 copy-start.2
  141.9 3.5 %copy-start.1 = (f32[2,4,256,128]{3,2,1,0:T(8,128)S(1)}, f32[2,4,256,128]{3,2,1,0:T(8,128)}, u32[]{:S(2)}) copy-start(f32[2,4,256,128]{3,2,1,0:T(8,128)} %get-tuple-element.124) | copy-start | bytes 3145732 | tf_op jit(solution)/shard_map/while/body/eval_jaxpr/cond
  149.5 1.0 copy-start.2
Sparse Core Ops, SparseCore 0:
  40.8 36.4 all-gather.2
  78.9 35.9 all-gather.4
where the time goes:
time: 161 us; the launch traced here: 160 us
  waiting for transfers between devices  65.4 us (41%)
  blocking collectives  26 us (16%)
  matrix products  19.7 us (12%)
  between operations  16 us (10%)
  local copies, waits for them, and re-layouts  14.8 us (9%)
  other arithmetic  14.6 us (9%)
  loops' own time  3.9 us (2%)
    all_gather x1, waiting for transfers between devices, on_device(): value_piece = lax.all_gather(value_rows, 'blk', axis=0, tiled=True)  36 us
    all_gather x1, waiting for transfers between devices, on_device(): key_piece = lax.all_gather(key_rows, 'blk', axis=0, tiled=True)  29.3 us
    psum x1, blocking collectives, on_device(): latent = lax.psum(partial_latent, ('team', 'head')).astype(jnp.bfloat16)  26 us
    dot_general x3, matrix products, compute(): jnp.einsum('kgts,skd->kgtd', weights.astype(jnp.bfloat16), block_values,...  12.1 us
    unnamed x7, local copies, waits for them, and re-layouts  7.28 us
    reduce_sum x3, other arithmetic, compute(): row_sum = row_sum * factor + jnp.sum(weights, axis=-1)  6.09 us
    dot_general x3, matrix products, compute(): jnp.einsum('tkgd,skd->kgts', query_rows, block_keys, preferred_element_ty...  4.2 us
    another operation x1, loops' own time, attend(): result, _ = lax.scan(advance, running, (key_split, value_split, pos_split))  3.67 us
  transfers between devices with their start and end apart: 2, of which 2 were waited for; matrix products, arithmetic and copies ran while one was open for 5% of the time, Pallas kernels for 0%

commit v1 on v0

--- a/solution.py
+++ b/solution.py
@@ -116,8 +116,11 @@
         jnp.zeros((kv_heads, group_dev, query_dev), jnp.float32),
         jnp.zeros((kv_heads, group_dev, query_dev, head_dim), jnp.float32),
     )
-    key_piece = lax.all_gather(key_rows, "blk", axis=0, tiled=True)
-    value_piece = lax.all_gather(value_rows, "blk", axis=0, tiled=True)
+    key_piece, value_piece = jnp.split(
+        lax.all_gather(jnp.concatenate([key_rows, value_rows], axis=1), "blk", axis=0, tiled=True),
+        [key_rows.shape[1]],
+        axis=1,
+    )
     piece_pos = key_positions(
         key_piece.shape[0], shard_rows, prefix_dev, query_dev, block_order, block_count
     )

time: 161 us -> 153 us (0.950)
  waiting for transfers between devices: 65.4 us -> 58.5 us
    all_gather x2 -> x1, waiting for transfers between devices: 65.3 us -> 58.5 us  [on_device(): lax.all_gather(jnp.concatenate([key_rows, value_rows], axis=1), 'blk', ax...]
    unnamed x7, local copies, waits for them, and re-layouts: 7.28 us -> 4.45 us
    split x0 -> x1, local copies, waits for them, and re-layouts: none -> 2.08 us  [on_device(): jnp.split(lax.all_gather(jnp.concatenate([key_rows, value_rows], axis=1),...]
  transfers between devices with their start and end apart: 2 -> 1, of which waited for: 2 -> 1; matrix products, arithmetic and copies ran while one was open for 5% -> 3% of each run, Pallas kernels for 0% -> 0%
where the time goes in v1:
time: 153 us
  waiting for transfers between devices  58.5 us (38%)
  blocking collectives  26 us (17%)
  matrix products  19.7 us (13%)
  between operations  16.2 us (11%)
  local copies, waits for them, and re-layouts  14.1 us (9%)
  other arithmetic  14.1 us (9%)
  loops' own time  3.94 us (3%)
    all_gather x1, waiting for transfers between devices, on_device(): lax.all_gather(jnp.concatenate([key_rows, value_rows], axis=1), 'blk', ax...  58.5 us
    psum x1, blocking collectives, on_device(): latent = lax.psum(partial_latent, ('team', 'head')).astype(jnp.bfloat16)  26 us
    dot_general x3, matrix products, compute(): jnp.einsum('kgts,skd->kgtd', weights.astype(jnp.bfloat16), block_values,...  12.1 us
    reduce_sum x3, other arithmetic, compute(): row_sum = row_sum * factor + jnp.sum(weights, axis=-1)  6.09 us
    unnamed x7, local copies, waits for them, and re-layouts  4.45 us
    dot_general x3, matrix products, compute(): jnp.einsum('tkgd,skd->kgts', query_rows, block_keys, preferred_element_ty...  4.2 us
    another operation x1, loops' own time, attend(): result, _ = lax.scan(advance, running, (key_split, value_split, pos_split))  3.7 us
  transfers between devices with their start and end apart: 1, of which 1 were waited for; matrix products, arithmetic and copies ran while one was open for 3% of the time, Pallas kernels for 0%

profile of v1, /device:TPU:0, one launch (start us, length us, event | category | flops | bytes accessed | tf_op | source)
XLA Modules:
  0.0 152.6 jit_solution(7637905259982797117)
XLA Ops:
  6.5 0.0 copy-start
  6.5 0.0 all-gather.2.cloned.1.call-start
  6.5 1.4 dynamic_slice.39
  10.0 0.0 copy-done
  10.0 1.2 convolution_bitcast_fusion
  11.2 26.0 %psum.7 = bf16[256,64]{0,1:T(8,128)(2,1)S(1)} all-reduce(f32[256,64]{0,1:T(8,128)S(1)} %convolution_bitcast_fusion), channel_id=1, replica_groups=mesh['team'=2,'blk'=4,'head'=4] {'team','head'}, use_global_device_ids=true, to_apply=%region_0.1 | all-reduce | flops 16384 | bytes 98304 | tf_op jit(solution)/shard_map/psum | solution.py:98
  37.2 1.0 copy.35
  38.2 1.0 copy.38
  39.2 0.8 constant_dynamic-slice_fusion.1
  40.0 1.1 fusion.21
  41.1 1.1 fusion.22
  42.2 0.9 maximum_maximum_fusion
  43.2 0.0 all-gather.2.cloned.1.call-update
  43.2 1.3 dynamic_slice.38
  45.1 0.7 add_reduce_fusion
  45.8 1.1 copy.40
  46.9 0.8 select_reduce_fusion
  47.7 58.5 %all-gather.2.cloned.1.call-done = bf16[3072,4,128]{2,0,1:T(8,128)(2,1)} async-done(((bf16[768,4,128]{2,0,1:T(8,128)(2,1)}), bf16[3072,4,128]{2,0,1:T(8,128)(2,1)}) %all-gather.2.cloned.1.call-update) | async-done | bytes 3145744 | tf_op jit(solution)/shard_map/all_gather | solution.py:120
  106.2 2.1 %fusion.42 = (bf16[3072,2,128]{2,0,1:T(8,128)(2,1)S(1)}, bf16[3072,2,128]{2,0,1:T(8,128)(2,1)S(1)}) fusion(bf16[3072,4,128]{2,0,1:T(8,128)(2,1)} %all-gather.2.cloned.1.call-done), kind=kLoop, calls=%fused_computation.68 | loop fusion | bytes 6291456 | tf_op jit(solution)/shard_map/split | solution.py:119
  108.3 0.1 copy.39
  108.4 1.3 copy.41
  109.7 1.0 broadcast_in_dim.56
  110.7 31.9 %while.15 = (s32[]{:T(128)}, f32[2,4,256]{2,1,0:T(4,128)S(1)}, f32[2,4,256]{2,1,0:T(4,128)S(1)}, f32[2,4,256,128]{3,2,1,0:T(8,128)}, s32[3,1024]{1,0:T(4,128)S(1...) while((s32[]{:T(128)}, f32[2,4,256]{2,1,0:T(4,128)S(1)}, ...), condition=%wide.region_9.10_spmd.clone, body=%wide.region_3.9_spmd.clone.sunk | while | flops 1101796608 | bytes 38421312 | solution.py:69
  110.7 0.7 fusion.46
  112.6 8.7 %conditional.3 = (f32[2,4,256]{2,1,0:T(4,128)S(1)}, f32[2,4,256]{2,1,0:T(4,128)S(1)}, f32[2,4,256,128]{3,2,1,0:T(8,128)}) conditional(s32[]{:T(128)} %convert_element_type.57, (s32[1,1024]{1,0:T(1,128)S(1)}, s32[]{:T(128)}, bf16[3,1024,2,128]{3,1,2,0:T(8,128)(2,1)S(1)}, s32[]{:T(128)}, bf16[256,2,4,128]{3,0,2,1:T(8,128)(2,1)S(1)}, ...), branch_computations={%region_5.7_spmd, %region_8.8_spmd} | conditional | flops 1101795584 | bytes 38395480 | solution.py:67
  112.6 0.2 broadcast_compare_fusion
  112.8 0.0 copy-start.1
  112.8 1.4 fusion.2
  114.3 2.0 %fusion.4 = f32[2,4,256]{2,1,0:T(4,128)S(1)} fusion(f32[2,1024,256,4]{2,1,3,0:T(8,128)S(1)} %get-tuple-element.228, f32[2,4,256]{2,1,0:T(4,128)S(1)} %max.4, pred[256,1024]{0,1:T(8,128)(4,1)S(1)} %broadcast_compare_fusion), kind=kLoop, calls=%fused_computation.5 | loop fusion | flops 10483712 | bytes 8667136 | tf_op jit(solution)/shard_map/while/body/eval_jaxpr/cond/branch_0_fun/reduce_sum | solution.py:57
  116.3 0.0 copy-done.1
  116.3 4.0 %fusion.8 = f32[2,4,256,128]{3,2,1,0:T(8,128)S(1)} fusion(f32[2,1024,256,4]{2,1,3,0:T(8,128)S(1)} %get-tuple-element.228, f32[2,4,256]{2,1,0:T(4,128)S(1)} %max.4, pred[256,1024]{0,1:T(8,128)(4,1)S(1)} %broadcast_compare_fusion, f32[2,4,256,128]{3,2,1,0:T(8,128)S(1)} %copy-done.1, bf16[3,1024,2,128]{3,1,2,0:T(8,128)(2,1)} %get-tuple-element.125, ...), kind=kOutput, calls=%fused_computation.8 | convolution fusion | flops 547880960 | bytes 11289088 | tf_op jit(solution)/shard_map/while/body/eval_jaxpr/cond/branch_0_fun/kgts,skd->kgtd/dot_general | solution.py:58
  120.4 0.0 copy-start.2
  120.4 1.0 copy-done.2
  121.3 0.7 fusion.46
  123.2 8.7 %conditional.3 = (f32[2,4,256]{2,1,0:T(4,128)S(1)}, f32[2,4,256]{2,1,0:T(4,128)S(1)}, f32[2,4,256,128]{3,2,1,0:T(8,128)}) conditional(s32[]{:T(128)} %convert_element_type.57, (s32[1,1024]{1,0:T(1,128)S(1)}, s32[]{:T(128)}, bf16[3,1024,2,128]{3,1,2,0:T(8,128)(2,1)S(1)}, s32[]{:T(128)}, bf16[256,2,4,128]{3,0,2,1:T(8,128)(2,1)S(1)}, ...), branch_computations={%region_5.7_spmd, %region_8.8_spmd} | conditional | flops 1101795584 | bytes 38395480 | solution.py:67
  123.2 0.2 broadcast_compare_fusion
  123.5 0.0 copy-start.1
  123.5 1.4 fusion.2
  124.9 2.0 %fusion.4 = f32[2,4,256]{2,1,0:T(4,128)S(1)} fusion(f32[2,1024,256,4]{2,1,3,0:T(8,128)S(1)} %get-tuple-element.228, f32[2,4,256]{2,1,0:T(4,128)S(1)} %max.4, pred[256,1024]{0,1:T(8,128)(4,1)S(1)} %broadcast_compare_fusion), kind=kLoop, calls=%fused_computation.5 | loop fusion | flops 10483712 | bytes 8667136 | tf_op jit(solution)/shard_map/while/body/eval_jaxpr/cond/branch_0_fun/reduce_sum | solution.py:57
  126.9 0.0 copy-done.1
  127.0 4.0 %fusion.8 = f32[2,4,256,128]{3,2,1,0:T(8,128)S(1)} fusion(f32[2,1024,256,4]{2,1,3,0:T(8,128)S(1)} %get-tuple-element.228, f32[2,4,256]{2,1,0:T(4,128)S(1)} %max.4, pred[256,1024]{0,1:T(8,128)(4,1)S(1)} %broadcast_compare_fusion, f32[2,4,256,128]{3,2,1,0:T(8,128)S(1)} %copy-done.1, bf16[3,1024,2,128]{3,1,2,0:T(8,128)(2,1)} %get-tuple-element.125, ...), kind=kOutput, calls=%fused_computation.8 | convolution fusion | flops 547880960 | bytes 11289088 | tf_op jit(solution)/shard_map/while/body/eval_jaxpr/cond/branch_0_fun/kgts,skd->kgtd/dot_general | solution.py:58
  131.0 0.0 copy-start.2
  131.0 1.0 copy-done.2
  132.0 0.7 fusion.46
  133.8 8.7 %conditional.3 = (f32[2,4,256]{2,1,0:T(4,128)S(1)}, f32[2,4,256]{2,1,0:T(4,128)S(1)}, f32[2,4,256,128]{3,2,1,0:T(8,128)}) conditional(s32[]{:T(128)} %convert_element_type.57, (s32[1,1024]{1,0:T(1,128)S(1)}, s32[]{:T(128)}, bf16[3,1024,2,128]{3,1,2,0:T(8,128)(2,1)S(1)}, s32[]{:T(128)}, bf16[256,2,4,128]{3,0,2,1:T(8,128)(2,1)S(1)}, ...), branch_computations={%region_5.7_spmd, %region_8.8_spmd} | conditional | flops 1101795584 | bytes 38395480 | solution.py:67
  133.9 0.2 broadcast_compare_fusion
  134.1 0.0 copy-start.1
  134.1 1.4 fusion.2
  135.5 2.0 %fusion.4 = f32[2,4,256]{2,1,0:T(4,128)S(1)} fusion(f32[2,1024,256,4]{2,1,3,0:T(8,128)S(1)} %get-tuple-element.228, f32[2,4,256]{2,1,0:T(4,128)S(1)} %max.4, pred[256,1024]{0,1:T(8,128)(4,1)S(1)} %broadcast_compare_fusion), kind=kLoop, calls=%fused_computation.5 | loop fusion | flops 10483712 | bytes 8667136 | tf_op jit(solution)/shard_map/while/body/eval_jaxpr/cond/branch_0_fun/reduce_sum | solution.py:57
  137.6 0.0 copy-done.1
  137.6 4.0 %fusion.8 = f32[2,4,256,128]{3,2,1,0:T(8,128)S(1)} fusion(f32[2,1024,256,4]{2,1,3,0:T(8,128)S(1)} %get-tuple-element.228, f32[2,4,256]{2,1,0:T(4,128)S(1)} %max.4, pred[256,1024]{0,1:T(8,128)(4,1)S(1)} %broadcast_compare_fusion, f32[2,4,256,128]{3,2,1,0:T(8,128)S(1)} %copy-done.1, bf16[3,1024,2,128]{3,1,2,0:T(8,128)(2,1)} %get-tuple-element.125, ...), kind=kOutput, calls=%fused_computation.8 | convolution fusion | flops 547880960 | bytes 11289088 | tf_op jit(solution)/shard_map/while/body/eval_jaxpr/cond/branch_0_fun/kgts,skd->kgtd/dot_general | solution.py:58
  141.6 0.0 copy-start.2
  141.6 1.0 copy-done.2
  142.6 0.2 copy.42
  142.8 2.9 %fusion.24 = bf16[256,2,4,128]{3,2,1,0:T(4,128)(2,1)} fusion(f32[2,4,256]{1,0,2:T(2,128)S(1)} %copy.42, f32[2,4,256,128]{3,2,1,0:T(8,128)} %get-tuple-element.142), kind=kLoop, calls=%fused_computation.32 | loop fusion | flops 524288 | bytes 1581056 | tf_op jit(solution)/shard_map/convert_element_type | solution.py:131
  (21 shorter events, 0.1 us)
Async XLA Ops:
  6.5 3.5 %copy-start = (bf16[256,1024]{1,0:T(8,128)(2,1)S(1)}, bf16[256,1024]{1,0:T(8,128)(2,1)}, u32[]{:S(2)}) copy-start(bf16[256,1024]{1,0:T(8,128)(2,1)} %param.16) | copy-start | bytes 1572868
  6.5 99.7 %all-gather.2.cloned.1.call-start = ((), (), s32[]{:S(2)}) async-start(), calls=%async_computation | async-start | bytes 3932160 | tf_op jit(solution)/shard_map/all_gather | solution.py:120
  112.8 3.5 %copy-start.1 = (f32[2,4,256,128]{3,2,1,0:T(8,128)S(1)}, f32[2,4,256,128]{3,2,1,0:T(8,128)}, u32[]{:S(2)}) copy-start(f32[2,4,256,128]{3,2,1,0:T(8,128)} %get-tuple-element.124) | copy-start | bytes 3145732 | tf_op jit(solution)/shard_map/while/body/eval_jaxpr/cond
  120.4 1.0 copy-start.2
  123.5 3.5 %copy-start.1 = (f32[2,4,256,128]{3,2,1,0:T(8,128)S(1)}, f32[2,4,256,128]{3,2,1,0:T(8,128)}, u32[]{:S(2)}) copy-start(f32[2,4,256,128]{3,2,1,0:T(8,128)} %get-tuple-element.124) | copy-start | bytes 3145732 | tf_op jit(solution)/shard_map/while/body/eval_jaxpr/cond
  131.0 1.0 copy-start.2
  134.1 3.5 %copy-start.1 = (f32[2,4,256,128]{3,2,1,0:T(8,128)S(1)}, f32[2,4,256,128]{3,2,1,0:T(8,128)}, u32[]{:S(2)}) copy-start(f32[2,4,256,128]{3,2,1,0:T(8,128)} %get-tuple-element.124) | copy-start | bytes 3145732 | tf_op jit(solution)/shard_map/while/body/eval_jaxpr/cond
  141.6 1.0 copy-start.2
Sparse Core Ops, SparseCore 0:
  43.3 62.8 all-gather.1
